TPU v7x, 512 devices: a whole 4x8x8 slice. The times are simulated.
512 devices in a mesh: grid: 16 (over y, core), tile: 32 (over x, z).
Axes of the slice: x: 4, y: 8, z: 8, core: 2. Of those that a mesh axis runs over, the one named last changes fastest.
Arguments:
- rhs_local: bfloat16 [192, 786432], P(None, ('grid', 'tile')), may hold values from -6 to 6
- diag_inv: bfloat16 [1536, 512, 512], P(('grid', 'tile')), may hold values from -1 to 2, as said below
- codes: bfloat16 [327680, 1536], P(('grid', 'tile')), may hold values from -127 to 127, as said below
- row_scales: float32 [327680], P(('grid', 'tile')), may hold values from 0 to 1, as said below
- sep_index: int32 [327680], P(('grid', 'tile')), may hold values from 0 to 2559, as said below
- live_rows: int32 [512], P(('grid', 'tile')), may hold values from 160 to 640, as said below
- rhs_sep: bfloat16 [192, 2560], P(None, 'tile'), may hold values from -6 to 6
- root_inv: bfloat16 [2560, 2560], P('tile'), may hold values from -1 to 2, as said below
Outputs:
- solution_local: bfloat16 [192, 786432], P(None, ('grid', 'tile'))
- solution_sep: float32 [192, 2560], P(None, 'tile')
Inputs may be any that keep to these rules, and one draw needn't show every extreme that they name: `diag_inv`: each block is upper triangular. `root_inv`: each block is upper triangular. `codes`: Integers. `row_scales`: Positive. `sep_index`: of each device's 640 entries, the j-th run of 20 consecutive entries lies in j * 80 to (j + 1) * 80 - 1, and the entries of one run are distinct. `live_rows`: some device has all 640 rows live.
All inputs are finite; a program needn't handle non-finite values.
Results may differ from a plain program's by a relative error of at most 0.0054.
Values may be sent and summed in bfloat16 or wider, within the bound.
No kernel may reach another device: no remote copies, remote signals or barrier semaphores. Data moves between devices by JAX's collectives and lax.ppermute only.
A program may use at most 64 MiB of HBM per device.

v0:
```python
import jax
import jax.numpy as jnp
from jax import lax
from jax.sharding import PartitionSpec as P


def selector(offsets, share_len):
    columns = jnp.arange(share_len, dtype=jnp.int32)
    return (offsets[:, :, None] == columns[None, None, :]).astype(jnp.float32)


def on_device(rhs_local, diag_inv, codes, row_scales, sep_index, live_rows, rhs_sep, root_inv):
    rhs_count, local_len = rhs_local.shape
    per_dev, block_len = (diag_inv.shape[0], diag_inv.shape[1])
    coupled_rows = codes.shape[0]
    share_len, sep_len = root_inv.shape
    tile_count = lax.axis_size("tile")
    per_share = coupled_rows // tile_count
    pieces = []
    for block_pos in range(per_dev):
        columns = rhs_local[:, block_pos * block_len : (block_pos + 1) * block_len]
        pieces.append(jnp.dot(columns, diag_inv[block_pos], preferred_element_type=jnp.float32))
    forward_flat = jnp.concatenate(pieces, axis=1).astype(jnp.bfloat16)
    positions = jnp.arange(coupled_rows, dtype=jnp.int32)
    row_factor = row_scales * (positions < live_rows[0]).astype(jnp.float32)
    coupled = (
        lax.dot_general(
            forward_flat, codes, (((1,), (1,)), ((), ())), preferred_element_type=jnp.float32
        )
        * row_factor[None, :]
    )
    bases = (jnp.arange(tile_count, dtype=jnp.int32) * share_len)[:, None]
    local_offsets = sep_index.reshape(tile_count, per_share) - bases
    onehot = selector(local_offsets, share_len)
    values = coupled.reshape(rhs_count, tile_count, per_share)
    partial_value = jnp.einsum(
        "rjp,jps->rjs", values, onehot, precision=lax.Precision.HIGHEST
    ).reshape(rhs_count, sep_len)
    summed = lax.psum(partial_value, ("grid", "tile"))
    own_share = lax.dynamic_slice_in_dim(summed, lax.axis_index("tile") * share_len, share_len, 1)
    residue = (rhs_sep.astype(jnp.float32) - own_share).astype(jnp.bfloat16)
    root_part = jnp.dot(residue, root_inv, preferred_element_type=jnp.float32)
    forward_sep = lax.psum(root_part, "tile").astype(jnp.bfloat16)
    solved = lax.dot_general(
        forward_sep, root_inv, (((1,), (1,)), ((), ())), preferred_element_type=jnp.float32
    )
    gathered = lax.all_gather(solved.astype(jnp.bfloat16), "tile", axis=1, tiled=True)
    gathered_split = gathered.astype(jnp.float32).reshape(rhs_count, tile_count, share_len)
    picked = jnp.einsum(
        "rjs,jps->rjp", gathered_split, onehot, precision=lax.Precision.HIGHEST
    ).reshape(rhs_count, coupled_rows)
    weighted = (picked * row_factor[None, :]).astype(jnp.bfloat16)
    update = jnp.dot(weighted, codes, preferred_element_type=jnp.float32)
    misfit = (forward_flat.astype(jnp.float32) - update).astype(jnp.bfloat16)
    results = []
    for block_pos in range(per_dev):
        columns = misfit[:, block_pos * block_len : (block_pos + 1) * block_len]
        results.append(
            lax.dot_general(
                columns,
                diag_inv[block_pos],
                (((1,), (1,)), ((), ())),
                preferred_element_type=jnp.float32,
            )
        )
    result = jnp.concatenate(results, axis=1)
    return (result.astype(jnp.bfloat16), solved)


def solution(mesh):
    return jax.shard_map(
        on_device,
        mesh=mesh,
        in_specs=(
            P(None, ("grid", "tile")),
            P(("grid", "tile"), None, None),
            P(("grid", "tile"), None),
            P(("grid", "tile")),
            P(("grid", "tile")),
            P(("grid", "tile")),
            P(None, "tile"),
            P("tile", None),
        ),
        out_specs=(P(None, ("grid", "tile")), P(None, "tile")),
        check_vma=False,
    )
```

profile of v0, /device:TPU:34, one launch (start us, length us, event | category | flops | bytes accessed | tf_op | source)
XLA Modules:
  0.0 530.7 jit_solution(14506760942146203309)
XLA Ops:
  7.2 0.0 copy-start
  7.2 0.0 copy-start.4
  7.2 0.0 all-reduce.3.cloned.1.call-start
  7.2 1.5 convolution_convert_fusion.3
  8.8 0.0 copy-start.6
  8.8 1.5 convolution_convert_fusion.4
  10.3 0.0 copy-start.7
  10.3 1.5 convolution_convert_fusion.5
  11.8 0.0 copy-start.8
  12.4 0.0 copy-done.4
  12.5 0.0 copy-done.6
  12.5 0.0 copy-done.7
  12.5 0.0 copy-done.8
  12.5 0.0 copy-done
  12.5 0.8 convolution_multiply_fusion
  13.3 0.0 copy-start.3
  13.3 0.2 copy.12
  13.6 0.1 reshape.44
  13.6 0.4 copy-done.3
  14.0 0.1 reshape.43
  14.1 0.1 broadcast_subtract_fusion
  14.2 3.0 fusion.15
  17.1 0.0 copy-start.1
  17.1 0.0 copy-start.2
  17.1 0.0 all-reduce.3.cloned.1.call-update
  17.2 285.0 %all-reduce.3.cloned.1.call-done = f32[192,2560]{0,1:T(8,128)} async-done(((f32[192,2560]{0,1:T(8,128)}), f32[192,2560]{0,1:T(8,128)}) %all-reduce.3.cloned.1.call-update) | async-done | bytes 1966096 | tf_op jit(solution)/shard_map/psum | solution.py:39
  302.1 0.0 copy-done.1
  302.2 0.0 copy-done.2
  302.2 2.6 fusion.25
  304.8 154.0 %all-reduce.4 = bf16[192,2560]{1,0:T(8,128)(2,1)S(1)} all-reduce(f32[192,2560]{1,0:T(8,128)} %fusion.25), channel_id=1, replica_groups=mesh['grid'=16,'tile'=32] {'tile'}, use_global_device_ids=true, to_apply=%region_1.0 | all-reduce | flops 491520 | bytes 2949120 | tf_op jit(solution)/shard_map/psum | solution.py:43
  458.8 1.1 fusion.29
  459.8 59.6 %all_gather.3 = bf16[192,2560]{0,1:T(8,128)(2,1)S(1)} all-gather(bf16[192,80]{0,1:T(8,128)(2,1)S(1)} %get-tuple-element.2), channel_id=1, replica_groups=mesh['grid'=16,'tile'=32] {'tile'}, dimensions={1}, use_global_device_ids=true | all-gather | bytes 1013760 | tf_op jit(solution)/shard_map/all_gather | solution.py:47
  519.5 0.4 convolution_bitcast_fusion
  519.8 0.1 reshape.47
  519.9 0.2 copy.13
  520.1 0.0 copy-start.5
  520.1 1.9 fusion
  522.0 0.0 copy-done.5
  522.0 0.3 convolution_convert_fusion
  522.4 0.3 convolution_convert_fusion.1
  522.7 0.3 convolution_convert_fusion.2
  523.0 0.9 pad_maximum_fusion.1
  (2 shorter events, 0.0 us)
Async XLA Ops:
  7.2 5.3 %copy-start = (bf16[640,1536]{1,0:T(8,128)(2,1)S(1)}, bf16[640,1536]{1,0:T(8,128)(2,1)}, u32[]{:S(2)}) copy-start(bf16[640,1536]{1,0:T(8,128)(2,1)} %param.10) | copy-start | bytes 5898244
  7.2 5.3 copy-start.4
  7.2 295.0 %all-reduce.3.cloned.1.call-start = ((), (), s32[]{:S(2)}) async-start(), calls=%async_computation | async-start | bytes 5242880 | tf_op jit(solution)/shard_map/psum | solution.py:39
  8.8 3.7 copy-start.6
  10.3 2.2 copy-start.7
  11.8 0.7 copy-start.8
  13.3 0.7 copy-start.3
  17.1 285.0 %copy-start.1 = (bf16[80,2560]{1,0:T(8,128)(2,1)S(1)}, bf16[80,2560]{1,0:T(8,128)(2,1)}, u32[]{:S(2)}) copy-start(bf16[80,2560]{1,0:T(8,128)(2,1)} %param.15) | copy-start | bytes 1228804
  17.1 285.0 %copy-start.2 = (bf16[192,80]{0,1:T(8,128)(2,1)S(1)}, bf16[192,80]{0,1:T(8,128)(2,1)}, u32[]{:S(2)}) copy-start(bf16[192,80]{0,1:T(8,128)(2,1)} %param.14) | copy-start | bytes 92164
  520.1 1.9 copy-start.5
Sparse Core Ops, SparseCore 0:
  17.3 284.8 all-reduce.2
where the time goes:
time: 531 us
  waiting for transfers between devices  285 us (54%)
  blocking collectives  214 us (40%)
  matrix products  15.1 us (3%)
  between operations  14.9 us (3%)
    psum x1, waiting for transfers between devices, on_device(): summed = lax.psum(partial_value, ('grid', 'tile'))  285 us
    psum x1, blocking collectives, on_device(): forward_sep = lax.psum(root_part, 'tile').astype(jnp.bfloat16)  154 us
    all_gather x1, blocking collectives, on_device(): lax.all_gather(solved.astype(jnp.bfloat16), 'tile', axis=1, tiled=True)  59.6 us
  transfers between devices with their start and end apart: 1, of which 1 were waited for; matrix products, arithmetic and copies ran while one was open for 0% of the time, Pallas kernels for 0%

commit v1 on v0

--- a/solution.py
+++ b/solution.py
@@ -36,7 +36,7 @@
     partial_value = jnp.einsum(
         "rjp,jps->rjs", values, onehot, precision=lax.Precision.HIGHEST
     ).reshape(rhs_count, sep_len)
-    summed = lax.psum(partial_value, ("grid", "tile"))
+    summed = lax.psum(lax.psum(partial_value, "grid"), "tile")
     own_share = lax.dynamic_slice_in_dim(summed, lax.axis_index("tile") * share_len, share_len, 1)
     residue = (rhs_sep.astype(jnp.float32) - own_share).astype(jnp.bfloat16)
     root_part = jnp.dot(residue, root_inv, preferred_element_type=jnp.float32)

time: 531 us -> 544 us (1.024)
  the two profiles are of different devices: /device:TPU:34 before, /device:TPU:10 now
where the time goes in v1:
time: 544 us; the launch traced here: 543 us
  waiting for transfers between devices  298 us (55%)
  blocking collectives  214 us (39%)
  matrix products  15.2 us (3%)
  between operations  15 us (3%)
    psum x2, waiting for transfers between devices, on_device(): summed = lax.psum(lax.psum(partial_value, 'grid'), 'tile')  298 us
    psum x1, blocking collectives, on_device(): forward_sep = lax.psum(root_part, 'tile').astype(jnp.bfloat16)  154 us
    all_gather x1, blocking collectives, on_device(): lax.all_gather(solved.astype(jnp.bfloat16), 'tile', axis=1, tiled=True)  59.8 us
  transfers between devices with their start and end apart: 2, of which 2 were waited for; matrix products, arithmetic and copies ran while one was open for 0% of the time, Pallas kernels for 0%

profile of v1, /device:TPU:10, one launch (start us, length us, event | category | flops | bytes accessed | tf_op | source)
XLA Modules:
  0.0 543.4 jit_solution(18255381456391957552)
XLA Ops:
  7.2 0.0 copy-start
  7.2 0.0 copy-start.4
  7.2 0.0 all-reduce.4.cloned.1.call-start
  7.2 1.5 convolution_convert_fusion.3
  8.8 0.0 copy-start.6
  8.8 1.5 convolution_convert_fusion.4
  10.3 0.0 copy-start.7
  10.3 1.5 convolution_convert_fusion.5
  11.8 0.0 copy-start.8
  12.4 0.0 copy-done.4
  12.5 0.0 copy-done.6
  12.5 0.0 copy-done.7
  12.5 0.0 copy-done.8
  12.5 0.0 copy-done
  12.5 0.8 convolution_multiply_fusion
  13.3 0.0 copy-start.3
  13.3 0.2 copy.12
  13.6 0.1 reshape.44
  13.6 0.4 copy-done.3
  14.0 0.1 reshape.43
  14.1 0.1 broadcast_subtract_fusion
  14.2 3.0 fusion.15
  17.1 0.0 all-reduce.4.cloned.1.call-update
  17.2 0.0 copy-start.1
  17.2 0.0 copy-start.2
  17.2 0.0 all-reduce.6.cloned.1.call-start
  17.2 123.9 %all-reduce.4.cloned.1.call-done = f32[192,2560]{0,1:T(8,128)} async-done(((f32[192,2560]{0,1:T(8,128)}), f32[192,2560]{0,1:T(8,128)}) %all-reduce.4.cloned.1.call-update) | async-done | bytes 1966096 | tf_op jit(solution)/shard_map/psum | solution.py:39
  141.1 0.0 all-reduce.6.cloned.1.call-update
  141.2 173.8 %all-reduce.6.cloned.1.call-done = f32[192,2560]{0,1:T(8,128)} async-done(((f32[192,2560]{0,1:T(8,128)}), f32[192,2560]{0,1:T(8,128)}) %all-reduce.6.cloned.1.call-update) | async-done | bytes 1966096 | tf_op jit(solution)/shard_map/psum | solution.py:39
  314.9 0.0 copy-done.1
  314.9 0.0 copy-done.2
  314.9 2.6 fusion.25
  317.6 153.7 %all-reduce.7 = bf16[192,2560]{1,0:T(8,128)(2,1)S(1)} all-reduce(f32[192,2560]{1,0:T(8,128)} %fusion.25), channel_id=1, replica_groups=mesh['grid'=16,'tile'=32] {'tile'}, use_global_device_ids=true, to_apply=%region_2.0 | all-reduce | flops 491520 | bytes 2949120 | tf_op jit(solution)/shard_map/psum | solution.py:43
  471.3 1.1 fusion.29
  472.4 59.8 %all_gather.3 = bf16[192,2560]{0,1:T(8,128)(2,1)S(1)} all-gather(bf16[192,80]{0,1:T(8,128)(2,1)S(1)} %get-tuple-element.2), channel_id=1, replica_groups=mesh['grid'=16,'tile'=32] {'tile'}, dimensions={1}, use_global_device_ids=true | all-gather | bytes 1013760 | tf_op jit(solution)/shard_map/all_gather | solution.py:47
  532.2 0.4 convolution_bitcast_fusion
  532.5 0.1 reshape.47
  532.6 0.2 copy.13
  532.8 0.0 copy-start.5
  532.9 1.9 fusion
  534.7 0.0 copy-done.5
  534.7 0.3 convolution_convert_fusion
  535.1 0.3 convolution_convert_fusion.1
  535.4 0.3 convolution_convert_fusion.2
  535.7 0.9 pad_maximum_fusion.1
  (2 shorter events, 0.0 us)
Async XLA Ops:
  7.2 5.3 copy-start
  7.2 5.3 copy-start.4
  7.2 133.9 %all-reduce.4.cloned.1.call-start = ((), (), s32[]{:S(2)}) async-start(), calls=%async_computation | async-start | bytes 5242880 | tf_op jit(solution)/shard_map/psum | solution.py:39
  8.8 3.7 copy-start.6
  10.3 2.2 copy-start.7
  11.8 0.7 copy-start.8
  13.3 0.7 copy-start.3
  17.2 297.8 %copy-start.1 = (bf16[80,2560]{1,0:T(8,128)(2,1)S(1)}, bf16[80,2560]{1,0:T(8,128)(2,1)}, u32[]{:S(2)}) copy-start(bf16[80,2560]{1,0:T(8,128)(2,1)} %param.15) | copy-start | bytes 1228804
  17.2 297.7 %copy-start.2 = (bf16[192,80]{0,1:T(8,128)(2,1)S(1)}, bf16[192,80]{0,1:T(8,128)(2,1)}, u32[]{:S(2)}) copy-start(bf16[192,80]{0,1:T(8,128)(2,1)} %param.14) | copy-start | bytes 92164
  17.2 297.7 %all-reduce.6.cloned.1.call-start = ((), (), s32[]{:S(2)}) async-start(), calls=%async_computation.1 | async-start | bytes 5242880 | tf_op jit(solution)/shard_map/psum | solution.py:39
  532.8 1.9 copy-start.5
Sparse Core Ops, SparseCore 0:
  17.3 123.8 all-reduce.3
  144.7 170.1 all-reduce.5

commit v2 on v0

--- a/solution.py
+++ b/solution.py
@@ -44,7 +44,12 @@
     solved = lax.dot_general(
         forward_sep, root_inv, (((1,), (1,)), ((), ())), preferred_element_type=jnp.float32
     )
-    gathered = lax.all_gather(solved.astype(jnp.bfloat16), "tile", axis=1, tiled=True)
+    gathered = jnp.concatenate(
+        lax.all_to_all(
+            jnp.stack([solved.astype(jnp.bfloat16)] * lax.axis_size("tile")), "tile", 0, 0
+        ),
+        axis=1,
+    )
     gathered_split = gathered.astype(jnp.float32).reshape(rhs_count, tile_count, share_len)
     picked = jnp.einsum(
         "rjs,jps->rjp", gathered_split, onehot, precision=lax.Precision.HIGHEST

time: 531 us -> 515 us (0.970)
  the two profiles are of different devices: /device:TPU:34 before, /device:TPU:64 now
where the time goes in v2:
time: 515 us; the launch traced here: 514 us
  waiting for transfers between devices  285 us (55%)
  blocking collectives  198 us (38%)
  matrix products  15.1 us (3%)
  between operations  14.9 us (3%)
    psum x1, waiting for transfers between devices, on_device(): summed = lax.psum(partial_value, ('grid', 'tile'))  285 us
    psum x1, blocking collectives, on_device(): forward_sep = lax.psum(root_part, 'tile').astype(jnp.bfloat16)  167 us
    all_to_all x1, blocking collectives, on_device(): lax.all_to_all(jnp.stack([solved.astype(jnp.bfloat16)] * lax.axis_size('t...  30.5 us
  transfers between devices with their start and end apart: 1, of which 1 were waited for; matrix products, arithmetic and copies ran while one was open for 0% of the time, Pallas kernels for 0%

profile of v2, /device:TPU:64, one launch (start us, length us, event | category | flops | bytes accessed | tf_op | source)
XLA Modules:
  0.0 514.4 jit_solution(1600668212604616154)
XLA Ops:
  7.2 0.0 copy-start
  7.2 0.0 copy-start.4
  7.2 0.0 all-reduce.3.cloned.1.call-start
  7.2 1.5 convolution_convert_fusion.3
  8.8 0.0 copy-start.6
  8.8 1.5 convolution_convert_fusion.4
  10.3 0.0 copy-start.7
  10.3 1.5 convolution_convert_fusion.5
  11.8 0.0 copy-start.8
  12.4 0.0 copy-done.4
  12.5 0.0 copy-done.6
  12.5 0.0 copy-done.7
  12.5 0.0 copy-done.8
  12.5 0.0 copy-done
  12.5 0.8 convolution_multiply_fusion
  13.3 0.0 copy-start.3
  13.3 0.2 copy.12
  13.6 0.1 reshape.49
  13.6 0.4 copy-done.3
  14.0 0.1 reshape.48
  14.1 0.1 broadcast_subtract_fusion
  14.2 3.0 fusion.20
  17.1 0.0 copy-start.1
  17.1 0.0 copy-start.2
  17.1 0.0 all-reduce.3.cloned.1.call-update
  17.2 284.6 %all-reduce.3.cloned.1.call-done = f32[192,2560]{0,1:T(8,128)} async-done(((f32[192,2560]{0,1:T(8,128)}), f32[192,2560]{0,1:T(8,128)}) %all-reduce.3.cloned.1.call-update) | async-done | bytes 1966096 | tf_op jit(solution)/shard_map/psum | solution.py:39
  301.7 0.0 copy-done.1
  301.7 0.0 copy-done.2
  301.7 2.6 fusion.30
  304.3 167.2 %all-reduce.4 = bf16[192,2560]{1,0:T(8,128)(2,1)S(1)} all-reduce(f32[192,2560]{1,0:T(8,128)} %fusion.30), channel_id=1, replica_groups=mesh['grid'=16,'tile'=32] {'tile'}, use_global_device_ids=true, to_apply=%region_1.0 | all-reduce | flops 491520 | bytes 2949120 | tf_op jit(solution)/shard_map/psum | solution.py:43
  471.6 1.1 fusion.34
  472.6 0.1 stack.2
  472.7 30.5 %all_to_all.5 = bf16[32,192,80]{1,2,0:T(8,128)(2,1)S(1)} all-to-all(bf16[32,192,80]{1,2,0:T(8,128)(2,1)S(1)} %stack.2), channel_id=1, replica_groups=mesh['grid'=16,'tile'=32] {'tile'}, dimensions={0} | all-to-all | bytes 1966080 | tf_op jit(solution)/shard_map/all_to_all | solution.py:48
  503.2 0.4 fusion.3
  503.5 0.1 reshape.52
  503.6 0.2 copy.13
  503.8 0.0 copy-start.5
  503.9 1.9 fusion
  505.7 0.0 copy-done.5
  505.8 0.3 convolution_convert_fusion
  506.1 0.3 convolution_convert_fusion.1
  506.4 0.3 convolution_convert_fusion.2
  506.7 0.9 pad_maximum_fusion.1
  (2 shorter events, 0.0 us)
Async XLA Ops:
  7.2 5.3 %copy-start = (bf16[640,1536]{1,0:T(8,128)(2,1)S(1)}, bf16[640,1536]{1,0:T(8,128)(2,1)}, u32[]{:S(2)}) copy-start(bf16[640,1536]{1,0:T(8,128)(2,1)} %param.10) | copy-start | bytes 5898244
  7.2 5.3 %copy-start.4 = (f32[640]{0:T(1024)S(1)}, f32[640]{0:T(1024)}, u32[]{:S(2)}) copy-start(f32[640]{0:T(1024)} %param.11) | copy-start | bytes 7684
  7.2 294.5 %all-reduce.3.cloned.1.call-start = ((), (), s32[]{:S(2)}) async-start(), calls=%async_computation.1 | async-start | bytes 5242880 | tf_op jit(solution)/shard_map/psum | solution.py:39
  8.8 3.7 copy-start.6
  10.3 2.2 copy-start.7
  11.8 0.7 copy-start.8
  13.3 0.7 copy-start.3
  17.1 284.6 %copy-start.1 = (bf16[80,2560]{1,0:T(8,128)(2,1)S(1)}, bf16[80,2560]{1,0:T(8,128)(2,1)}, u32[]{:S(2)}) copy-start(bf16[80,2560]{1,0:T(8,128)(2,1)} %param.15) | copy-start | bytes 1228804
  17.1 284.6 %copy-start.2 = (bf16[192,80]{0,1:T(8,128)(2,1)S(1)}, bf16[192,80]{0,1:T(8,128)(2,1)}, u32[]{:S(2)}) copy-start(bf16[192,80]{0,1:T(8,128)(2,1)} %param.14) | copy-start | bytes 92164
  503.8 1.9 copy-start.5
Sparse Core Ops, SparseCore 0:
  17.3 284.3 all-reduce.2
